TPU v7x, 32 devices: a whole 2x2x4 slice. The times are simulated.
32 devices in a mesh: groups: 2 (over y), gx: 8 (over z, x), gy: 2 (over core).
Axes of the slice: x: 2, y: 2, z: 4, core: 2. Of those that a mesh axis runs over, the one named last changes fastest.
Arguments:
- voxels: bfloat16 [16, 128, 128, 64], P(('groups', 'gx'), 'gy'), parts along dimension 0, may hold values from -6 to 6
- occupancy: int32 [16, 128, 128], P(('groups', 'gx'), 'gy'), parts along dimension 0, may hold values 0 or 1
- row_weights: bfloat16 [8, 64], P('gx'), may hold values from -2 to 2
- column_weights: bfloat16 [128, 64], P('gy'), may hold values from -0.5 to 0.5
- depth_weights: bfloat16 [128, 64], replicated, may hold values from -0.5 to 0.5
- plane_kernels: bfloat16 [3, 2, 3, 3, 64, 64], replicated, may hold values from -0.25 to 0.25
- expand_weight: bfloat16 [64, 128], replicated, may hold values from -0.75 to 0.75
- shrink_weight: bfloat16 [128, 64], replicated, may hold values from -1 to 1
Outputs:
- updated: bfloat16 [16, 128, 128, 64], P(('groups', 'gx'), 'gy'), parts along dimension 0
There are 2 independent parts, one for each index of `groups`. A program takes and returns all parts, laid end to end along the dimension named above; an argument that names none is the same for every part. Nothing has to cross between parts.
All inputs are finite; a program needn't handle non-finite values. No bound on the sum of `occupancy` on one device may be relied on, other than what follows from the above.
Results may differ from a plain program's by a relative error of at most 0.015.
Values may be sent and summed in bfloat16 or wider, within the bound.
A program may use at most 64 MiB of HBM per device.

v0:
```python
import jax
import jax.numpy as jnp
from jax import lax
from jax.sharding import PartitionSpec as P

product_scale = 8.0


def with_halo(cells, sides, width):
    for axis, dim in sides:
        count = lax.axis_size(axis)
        ends = count - 1
        head = lax.slice_in_dim(cells, 0, width, axis=dim)
        tail = lax.slice_in_dim(cells, cells.shape[dim] - width, cells.shape[dim], axis=dim)
        cells = jnp.concatenate(
            [
                lax.ppermute(tail, axis, [(i, (i + 1) % count) for i in range(ends)]),
                cells,
                lax.ppermute(head, axis, [((i + 1) % count, i) for i in range(ends)]),
            ],
            axis=dim,
        )
    return cells


def conv_valid(padded, kernel):
    rows = padded.shape[0] - 2
    cols = padded.shape[1] - 2
    total = jnp.zeros((rows, cols, kernel.shape[-1]), jnp.float32)
    for row_off in range(3):
        for col_off in range(3):
            window = padded[row_off : row_off + rows, col_off : col_off + cols]
            total = total + jnp.einsum(
                "ijc,co->ijo", window, kernel[row_off, col_off], preferred_element_type=jnp.float32
            )
    return total


def plane_block(plane, kernels, extend):
    inner = jax.nn.silu(conv_valid(extend(plane), kernels[0])).astype(jnp.bfloat16)
    return conv_valid(extend(inner), kernels[1]).astype(jnp.bfloat16)


def rim_xy(plane):
    return with_halo(plane, (("gx", 0), ("gy", 1)), 1)


def rim_xz(plane):
    padded = with_halo(plane, (("gx", 0),), 1)
    return jnp.pad(padded, ((0, 0), (1, 1), (0, 0)))


def rim_yz(plane):
    padded = with_halo(plane, (("gy", 0),), 1)
    return jnp.pad(padded, ((0, 0), (1, 1), (0, 0)))


def shards(
    voxels,
    occupancy,
    row_weights,
    column_weights,
    depth_weights,
    plane_kernels,
    expand_weight,
    shrink_weight,
):
    features = voxels * occupancy.astype(jnp.bfloat16)[..., None]
    xy_plane = jnp.einsum(
        "xyzc,zc->xyc", features, depth_weights, preferred_element_type=jnp.float32
    ).astype(jnp.bfloat16)
    xz_part = jnp.einsum(
        "xyzc,yc->xzc", features, column_weights, preferred_element_type=jnp.float32
    )
    yz_part = jnp.einsum("xyzc,xc->yzc", features, row_weights, preferred_element_type=jnp.float32)
    xy_out = plane_block(xy_plane, plane_kernels[0], rim_xy)
    xz_plane = lax.psum(xz_part, "gy").astype(jnp.bfloat16)
    xz_out = plane_block(xz_plane, plane_kernels[1], rim_xz)
    yz_plane = lax.psum(yz_part, "gx").astype(jnp.bfloat16)
    yz_out = plane_block(yz_plane, plane_kernels[2], rim_yz)
    product = xy_out.astype(jnp.float32)[:, :, None, :] * xz_out.astype(jnp.float32)[:, None, :, :]
    product = product * yz_out.astype(jnp.float32)[None, :, :, :]
    mixed = (product_scale * product).astype(jnp.bfloat16)
    hidden = jax.nn.silu(
        jnp.einsum("xyzc,ch->xyzh", mixed, expand_weight, preferred_element_type=jnp.float32)
    ).astype(jnp.bfloat16)
    branch = jnp.einsum("xyzh,hc->xyzc", hidden, shrink_weight, preferred_element_type=jnp.float32)
    return (features.astype(jnp.float32) + branch).astype(jnp.bfloat16)


def solution(mesh):
    in_specs = (
        P(("groups", "gx"), "gy", None, None),
        P(("groups", "gx"), "gy", None),
        P("gx", None),
        P("gy", None),
        P(),
        P(),
        P(),
        P(),
    )
    out_specs = P(("groups", "gx"), "gy", None, None)
    return jax.shard_map(shards, mesh=mesh, in_specs=in_specs, out_specs=out_specs, check_vma=False)
```

profile of v0, /device:TPU:0, one launch (start us, length us, event | category | flops | bytes accessed | tf_op | source)
XLA Modules:
  0.0 184.0 jit_solution(3502592490292366999)
XLA Ops:
  0.0 0.7 bitcast_convert_fusion
  0.7 0.8 convert_bitcast_fusion
  1.4 1.7 convert_multiply_fusion
  3.2 0.8 fusion.67
  3.9 1.3 collective-permute-start.1
  5.2 5.5 %collective-permute-start = (bf16[1,64,64]{1,2,0:T(8,128)(2,1)S(1)}, bf16[1,64,64]{1,2,0:T(8,128)(2,1)S(1)}, u32[]{:S(2)}, u32[]{:S(2)}) collective-permute-start(bf16[1,64,64]{1,2,0:T(8,128)(2,1)S(1)} %convert_bitcast_fusion.1), channel_id=1, source_target_pairs={{0,2},{2,4},{4,6},{6,8},{8,10},{10,12},{12,14},{1,3},{3,5},{5,7},{... | collective-permute-start | bytes 24584 | tf_op jit(solution)/shard_map/ppermute | solution.py:17
  10.8 0.8 fusion.65
  11.6 3.4 %psum.14 = bf16[1,128,64]{1,2,0:T(8,128)(2,1)S(1)} all-reduce(f32[1,128,64]{1,2,0:T(8,128)S(1)} %bitcast.374), channel_id=1, replica_groups=mesh['groups'=2,'gx'=8,'gy'=2] {'gy'}, use_global_device_ids=true, to_apply=%region_0.1 | all-reduce | flops 8192 | bytes 49152 | tf_op jit(solution)/shard_map/psum | solution.py:77
  15.0 1.3 collective-permute-start.9
  16.3 6.1 %collective-permute-start.8 = (bf16[1,128,64]{1,2,0:T(8,128)(2,1)S(1)}, bf16[1,128,64]{1,2,0:T(8,128)(2,1)}, u32[]{:S(2)}, u32[]{:S(2)}) collective-permute-start(bf16[1,128,64]{1,2,0:T(8,128)(2,1)S(1)} %psum.14), channel_id=1, source_target_pairs={{0,2},{2,4},{4,6},{6,8},{8,10},{10,12},{12,14},{1,3},{3,5},{5,7},{... | collective-permute-start | bytes 49160 | tf_op jit(solution)/shard_map/ppermute | solution.py:17
  22.4 91.9 %all-reduce.5 = bf16[64,128,64]{1,2,0:T(8,128)(2,1)S(1)} all-reduce(f32[64,128,64]{1,2,0:T(8,128)S(1)} %get-tuple-element.5), channel_id=1, replica_groups=mesh['groups'=2,'gx'=8,'gy'=2] {'gx'}, use_global_device_ids=true, to_apply=%region_1.2 | all-reduce | flops 524288 | bytes 3145728 | tf_op jit(solution)/shard_map/psum | solution.py:79
  114.3 1.3 collective-permute-start.12
  115.6 1.3 slice_bitcast_fusion.4
  117.1 0.4 fusion.77
  117.5 0.7 pad_maximum_fusion.4
  118.4 1.3 collective-permute-start.2
  119.7 1.3 collective-permute-start.3
  121.1 1.3 collective-permute-start.13
  122.4 0.4 collective-permute-done.3
  122.8 0.9 maximum_maximum_fusion
  123.7 0.2 fusion.119
  124.1 0.2 convolution_add_fusion.21
  124.7 0.2 convolution_add_fusion.18
  125.1 0.9 multiply_convert_fusion.6
  126.1 1.3 collective-permute-start.5
  127.5 4.5 %collective-permute-start.4 = (bf16[1,64,64]{2,1,0:T(8,128)(2,1)S(1)}, bf16[1,64,64]{2,1,0:T(8,128)(2,1)S(1)}, u32[]{:S(2)}, u32[]{:S(2)}) collective-permute-start(bf16[1,64,64]{2,1,0:T(8,128)(2,1)S(1)} %bitcast.352), channel_id=1, source_target_pairs={{0,2},{2,4},{4,6},{6,8},{8,10},{10,12},{12,14},{1,3},{3,5},{5,7},{... | collective-permute-start | bytes 24584 | tf_op jit(solution)/shard_map/ppermute | solution.py:17
  132.0 0.8 fusion.74
  133.1 0.2 fusion.80
  133.3 0.9 convolution_add_fusion.13
  134.2 0.2 convolution_add_fusion.12
  134.8 0.2 convolution_add_fusion.9
  135.3 0.9 multiply_convert_fusion.5
  136.2 1.3 collective-permute-start.11
  137.5 4.5 %collective-permute-start.10 = (bf16[1,128,64]{1,2,0:T(8,128)(2,1)S(1)}, bf16[1,128,64]{1,2,0:T(8,128)(2,1)S(1)}, u32[]{:S(2)}, u32[]{:S(2)}) collective-permute-start(bf16[1,128,64]{1,2,0:T(8,128)(2,1)S(1)} %bitcast.372), channel_id=1, source_target_pairs={{0,2},{2,4},{4,6},{6,8},{8,10},{10,12},{12,14},{1,3},{3,5},{5,7},{... | collective-permute-start | bytes 49160 | tf_op jit(solution)/shard_map/ppermute | solution.py:17
  142.1 1.2 fusion.5
  143.2 0.4 fusion.47
  143.7 0.5 fusion.49
  144.2 0.4 fusion.51
  144.6 0.5 fusion.53
  145.2 0.4 fusion.57
  145.6 0.4 fusion.45
  146.0 0.4 fusion.55
  146.4 1.6 multiply_convert_fusion.2
  148.0 1.6 collective-permute-start.14
  149.6 0.5 fusion.76
  150.1 1.3 collective-permute-start.15
  151.4 1.3 collective-permute-start.7
  153.0 1.5 collective-permute-done.7
  154.5 2.2 %collective-permute-start.6 = (bf16[3,1,64]{2,1,0:T(2,128)(2,1)S(1)}, bf16[3,1,64]{2,1,0:T(2,128)(2,1)S(1)}, u32[]{:S(2)}, u32[]{:S(2)}) collective-permute-start(bf16[3,1,64]{2,1,0:T(2,128)(2,1)S(1)} %get-tuple-element.17), channel_id=1, source_target_pairs={{0,1},{2,3},{4,5},{6,7},{8,9},{10,11},{12,13},{14,15},{16,17},{18,... | collective-permute-start | bytes 1160 | tf_op jit(solution)/shard_map/ppermute | solution.py:17
  157.0 0.4 collective-permute-done.6
  158.2 0.2 fusion.78
  158.4 1.2 select_maximum_fusion
  159.6 1.8 fusion.31
  161.4 1.9 %fusion.33 = f32[64,128,64]{1,2,0:T(8,128)} fusion(bf16[66,130,64]{1,2,0:T(8,128)(2,1)S(1)} %select_maximum_fusion, bf16[3,3,64,64]{3,2,1,0:T(8,128)(2,1)S(1)} %get-tuple-element.15), kind=kOutput, calls=%fused_computation.66 | convolution fusion | flops 67108864 | bytes 3162112 | tf_op jit(solution)/shard_map/ijc,co->ijo/dot_general | solution.py:33
  163.3 1.9 %fusion.35 = f32[64,128,64]{1,2,0:T(8,128)} fusion(bf16[66,130,64]{1,2,0:T(8,128)(2,1)S(1)} %select_maximum_fusion, bf16[3,3,64,64]{3,2,1,0:T(8,128)(2,1)S(1)} %get-tuple-element.15), kind=kOutput, calls=%fused_computation.68 | convolution fusion | flops 67108864 | bytes 3162112 | tf_op jit(solution)/shard_map/ijc,co->ijo/dot_general | solution.py:33
  165.2 1.9 %fusion.37 = f32[64,128,64]{1,2,0:T(8,128)} fusion(bf16[66,130,64]{1,2,0:T(8,128)(2,1)S(1)} %select_maximum_fusion, bf16[3,3,64,64]{3,2,1,0:T(8,128)(2,1)S(1)} %get-tuple-element.15), kind=kOutput, calls=%fused_computation.70 | convolution fusion | flops 67108864 | bytes 3162112 | tf_op jit(solution)/shard_map/ijc,co->ijo/dot_general | solution.py:33
  167.1 1.8 fusion.39
  168.9 1.9 %fusion.29 = f32[64,128,64]{1,2,0:T(8,128)} fusion(bf16[66,130,64]{1,2,0:T(8,128)(2,1)S(1)} %select_maximum_fusion, bf16[3,3,64,64]{3,2,1,0:T(8,128)(2,1)S(1)} %get-tuple-element.15), kind=kOutput, calls=%fused_computation.62 | convolution fusion | flops 67108864 | bytes 3162112 | tf_op jit(solution)/shard_map/ijc,co->ijo/dot_general | solution.py:33
  171.0 0.2 convolution_add_fusion.5
  171.6 0.2 convolution_add_fusion.2
  172.0 1.8 fusion.25
  173.8 1.8 fusion.21
  175.6 0.2 fusion.20
  175.8 8.2 %fusion.6 = bf16[1,64,128,64]{2,3,1,0:T(8,128)(2,1)} fusion(f32[64,128,64]{1,2,0:T(8,128)} %fusion.29, f32[64,128,64]{1,2,0:T(8,128)} %fusion.25, f32[64,128,64]{1,2,0:T(8,128)} %fusion.31, f32[64,128,64]{1,2,0:T(8,128)} %fusion.33, f32[64,128,64]{1,2,0:T(8,128)S(1)} %fusion.76, f32[64,128,64]{1,2,0:T(8,128)} %fusion.35, f32[64,128,64]{1,2,0:T(8,128)} %fusion.37, ...), kind=kOutput, calls=%fused_computation.12 | convolution fusion | flops 284164096 | bytes 21069824 | tf_op jit(solution)/shard_map/xyzh,hc->xyzc/dot_general | solution.py:87
  (52 shorter events, 4.3 us)
Async XLA Ops:
  0.0 175.8 %copy-start = (bf16[128,64]{0,1:T(8,128)(2,1)S(1)}, bf16[128,64]{0,1:T(8,128)(2,1)}, u32[]{:S(2)}) copy-start(bf16[128,64]{0,1:T(8,128)(2,1)} %param.15) | copy-start | bytes 49156
  1.4 1.7 copy-start.3
  1.4 9.3 %copy-start.2 = (bf16[64,64]{1,0:T(8,128)(2,1)S(1)}, bf16[64,64]{1,0:T(8,128)(2,1)}, u32[]{:S(2)}) copy-start(bf16[64,64]{1,0:T(8,128)(2,1)} %param.11) | copy-start | bytes 24580
  3.9 113.6 %collective-permute-start.1 = (bf16[1,64,64]{1,2,0:T(8,128)(2,1)S(1)}, bf16[1,64,64]{1,2,0:T(8,128)(2,1)}, u32[]{:S(2)}, u32[]{:S(2)}) collective-permute-start(bf16[1,64,64]{1,2,0:T(8,128)(2,1)S(1)} %convert_bitcast_fusion.1), channel_id=1, source_target_pairs={{2,0},{4,2},{6,4},{8,6},{10,8},{12,10},{14,12},{3,1},{5,3},{7,5},{... | collective-permute-start | bytes 24584 | tf_op jit(solution)/shard_map/ppermute | solution.py:19
  5.2 112.3 %collective-permute-start = (bf16[1,64,64]{1,2,0:T(8,128)(2,1)S(1)}, bf16[1,64,64]{1,2,0:T(8,128)(2,1)S(1)}, u32[]{:S(2)}, u32[]{:S(2)}) collective-permute-start(bf16[1,64,64]{1,2,0:T(8,128)(2,1)S(1)} %convert_bitcast_fusion.1), channel_id=1, source_target_pairs={{0,2},{2,4},{4,6},{6,8},{8,10},{10,12},{12,14},{1,3},{3,5},{5,7},{... | collective-permute-start | bytes 24584 | tf_op jit(solution)/shard_map/ppermute | solution.py:17
  15.0 112.4 %collective-permute-start.9 = (bf16[1,128,64]{1,2,0:T(8,128)(2,1)S(1)}, bf16[1,128,64]{1,2,0:T(8,128)(2,1)}, u32[]{:S(2)}, u32[]{:S(2)}) collective-permute-start(bf16[1,128,64]{1,2,0:T(8,128)(2,1)S(1)} %psum.14), channel_id=1, source_target_pairs={{2,0},{4,2},{6,4},{8,6},{10,8},{12,10},{14,12},{3,1},{5,3},{7,5},{... | collective-permute-start | bytes 49160 | tf_op jit(solution)/shard_map/ppermute | solution.py:19
  16.3 115.7 %collective-permute-start.8 = (bf16[1,128,64]{1,2,0:T(8,128)(2,1)S(1)}, bf16[1,128,64]{1,2,0:T(8,128)(2,1)}, u32[]{:S(2)}, u32[]{:S(2)}) collective-permute-start(bf16[1,128,64]{1,2,0:T(8,128)(2,1)S(1)} %psum.14), channel_id=1, source_target_pairs={{0,2},{2,4},{4,6},{6,8},{8,10},{10,12},{12,14},{1,3},{3,5},{5,7},{... | collective-permute-start | bytes 49160 | tf_op jit(solution)/shard_map/ppermute | solution.py:17
  114.3 23.2 %collective-permute-start.12 = (bf16[1,128,64]{1,2,0:T(8,128)(2,1)S(1)}, bf16[1,128,64]{1,2,0:T(8,128)(2,1)S(1)}, u32[]{:S(2)}, u32[]{:S(2)}) collective-permute-start(bf16[1,128,64]{1,2,0:T(8,128)(2,1)S(1)} %get-tuple-element.9), channel_id=1, source_target_pairs={{0,1},{2,3},{4,5},{6,7},{8,9},{10,11},{12,13},{14,15},{16,17},{18,... | collective-permute-start | bytes 49160 | tf_op jit(solution)/shard_map/ppermute | solution.py:17
  118.4 2.8 %collective-permute-start.2 = (bf16[3,1,64]{1,2,0:T(8,128)(2,1)S(1)}, bf16[3,1,64]{1,2,0:T(8,128)(2,1)S(1)}, u32[]{:S(2)}, u32[]{:S(2)}) collective-permute-start(bf16[3,1,64]{1,2,0:T(8,128)(2,1)S(1)} %get-tuple-element.21), channel_id=1, source_target_pairs={{0,1},{2,3},{4,5},{6,7},{8,9},{10,11},{12,13},{14,15},{16,17},{18,... | collective-permute-start | bytes 1160 | tf_op jit(solution)/shard_map/ppermute | solution.py:17
  119.7 3.1 %collective-permute-start.3 = (bf16[3,1,64]{1,2,0:T(8,128)(2,1)S(1)}, bf16[3,1,64]{1,2,0:T(8,128)(2,1)S(1)}, u32[]{:S(2)}, u32[]{:S(2)}) collective-permute-start(bf16[3,1,64]{1,2,0:T(8,128)(2,1)S(1)} %get-tuple-element.22), channel_id=1, source_target_pairs={{1,0},{3,2},{5,4},{7,6},{9,8},{11,10},{13,12},{15,14},{17,16},{19,... | collective-permute-start | bytes 1160 | tf_op jit(solution)/shard_map/ppermute | solution.py:19
  121.1 20.9 %collective-permute-start.13 = (bf16[1,128,64]{1,2,0:T(8,128)(2,1)S(1)}, bf16[1,128,64]{1,2,0:T(8,128)(2,1)S(1)}, u32[]{:S(2)}, u32[]{:S(2)}) collective-permute-start(bf16[1,128,64]{1,2,0:T(8,128)(2,1)S(1)} %get-tuple-element.10), channel_id=1, source_target_pairs={{1,0},{3,2},{5,4},{7,6},{9,8},{11,10},{13,12},{15,14},{17,16},{19,... | collective-permute-start | bytes 49160 | tf_op jit(solution)/shard_map/ppermute | solution.py:19
  126.1 24.0 %collective-permute-start.5 = (bf16[1,64,64]{2,1,0:T(8,128)(2,1)S(1)}, bf16[1,64,64]{2,1,0:T(8,128)(2,1)S(1)}, u32[]{:S(2)}, u32[]{:S(2)}) collective-permute-start(bf16[1,64,64]{2,1,0:T(8,128)(2,1)S(1)} %bitcast.351), channel_id=1, source_target_pairs={{2,0},{4,2},{6,4},{8,6},{10,8},{12,10},{14,12},{3,1},{5,3},{7,5},{... | collective-permute-start | bytes 24584 | tf_op jit(solution)/shard_map/ppermute | solution.py:19
  127.5 23.9 %collective-permute-start.4 = (bf16[1,64,64]{2,1,0:T(8,128)(2,1)S(1)}, bf16[1,64,64]{2,1,0:T(8,128)(2,1)S(1)}, u32[]{:S(2)}, u32[]{:S(2)}) collective-permute-start(bf16[1,64,64]{2,1,0:T(8,128)(2,1)S(1)} %bitcast.352), channel_id=1, source_target_pairs={{0,2},{2,4},{4,6},{6,8},{8,10},{10,12},{12,14},{1,3},{3,5},{5,7},{... | collective-permute-start | bytes 24584 | tf_op jit(solution)/shard_map/ppermute | solution.py:17
  136.2 21.7 %collective-permute-start.11 = (bf16[1,128,64]{1,2,0:T(8,128)(2,1)S(1)}, bf16[1,128,64]{1,2,0:T(8,128)(2,1)S(1)}, u32[]{:S(2)}, u32[]{:S(2)}) collective-permute-start(bf16[1,128,64]{1,2,0:T(8,128)(2,1)S(1)} %bitcast.371), channel_id=1, source_target_pairs={{2,0},{4,2},{6,4},{8,6},{10,8},{12,10},{14,12},{3,1},{5,3},{7,5},{... | collective-permute-start | bytes 49160 | tf_op jit(solution)/shard_map/ppermute | solution.py:19
  137.5 20.4 %collective-permute-start.10 = (bf16[1,128,64]{1,2,0:T(8,128)(2,1)S(1)}, bf16[1,128,64]{1,2,0:T(8,128)(2,1)S(1)}, u32[]{:S(2)}, u32[]{:S(2)}) collective-permute-start(bf16[1,128,64]{1,2,0:T(8,128)(2,1)S(1)} %bitcast.372), channel_id=1, source_target_pairs={{0,2},{2,4},{4,6},{6,8},{8,10},{10,12},{12,14},{1,3},{3,5},{5,7},{... | collective-permute-start | bytes 49160 | tf_op jit(solution)/shard_map/ppermute | solution.py:17
  148.0 10.4 %collective-permute-start.14 = (bf16[1,128,64]{1,2,0:T(8,128)(2,1)S(1)}, bf16[1,128,64]{1,2,0:T(8,128)(2,1)S(1)}, u32[]{:S(2)}, u32[]{:S(2)}) collective-permute-start(bf16[1,128,64]{1,2,0:T(8,128)(2,1)S(1)} %get-tuple-element.7), channel_id=1, source_target_pairs={{0,1},{2,3},{4,5},{6,7},{8,9},{10,11},{12,13},{14,15},{16,17},{18,... | collective-permute-start | bytes 49160 | tf_op jit(solution)/shard_map/ppermute | solution.py:17
  150.1 8.3 %collective-permute-start.15 = (bf16[1,128,64]{1,2,0:T(8,128)(2,1)S(1)}, bf16[1,128,64]{1,2,0:T(8,128)(2,1)S(1)}, u32[]{:S(2)}, u32[]{:S(2)}) collective-permute-start(bf16[1,128,64]{1,2,0:T(8,128)(2,1)S(1)} %get-tuple-element.8), channel_id=1, source_target_pairs={{1,0},{3,2},{5,4},{7,6},{9,8},{11,10},{13,12},{15,14},{17,16},{19,... | collective-permute-start | bytes 49160 | tf_op jit(solution)/shard_map/ppermute | solution.py:19
  151.4 3.1 %collective-permute-start.7 = (bf16[3,1,64]{2,1,0:T(2,128)(2,1)S(1)}, bf16[3,1,64]{2,1,0:T(2,128)(2,1)S(1)}, u32[]{:S(2)}, u32[]{:S(2)}) collective-permute-start(bf16[3,1,64]{2,1,0:T(2,128)(2,1)S(1)} %get-tuple-element.18), channel_id=1, source_target_pairs={{1,0},{3,2},{5,4},{7,6},{9,8},{11,10},{13,12},{15,14},{17,16},{19,... | collective-permute-start | bytes 1160 | tf_op jit(solution)/shard_map/ppermute | solution.py:19
  154.5 2.9 %collective-permute-start.6 = (bf16[3,1,64]{2,1,0:T(2,128)(2,1)S(1)}, bf16[3,1,64]{2,1,0:T(2,128)(2,1)S(1)}, u32[]{:S(2)}, u32[]{:S(2)}) collective-permute-start(bf16[3,1,64]{2,1,0:T(2,128)(2,1)S(1)} %get-tuple-element.17), channel_id=1, source_target_pairs={{0,1},{2,3},{4,5},{6,7},{8,9},{10,11},{12,13},{14,15},{16,17},{18,... | collective-permute-start | bytes 1160 | tf_op jit(solution)/shard_map/ppermute | solution.py:17
  173.8 2.0 %copy-start.1 = (bf16[1,64,128,64]{2,3,1,0:T(8,128)(2,1)S(1)}, bf16[1,64,128,64]{2,3,1,0:T(8,128)(2,1)}, u32[]{:S(2)}) copy-start(bf16[1,64,128,64]{2,3,1,0:T(8,128)(2,1)} %param.8) | copy-start | bytes 3145732
where the time goes:
time: 185 us; the launch traced here: 184 us
  blocking collectives  95.3 us (52%)
  matrix products  38.9 us (21%)
  starting transfers between devices  37.4 us (20%)
  other arithmetic  8.05 us (4%)
  waiting for transfers between devices  2.27 us (1%)
    psum x1, blocking collectives, shards(): yz_plane = lax.psum(yz_part, 'gx').astype(jnp.bfloat16)  91.9 us
    dot_general x54, matrix products, conv_valid(): jnp.einsum('ijc,co->ijo', window, kernel[row_off, col_off], preferred_ele...  29.1 us
    ppermute x8, starting transfers between devices, with_halo(): lax.ppermute(tail, axis, [(i, (i + 1) % count) for i in range(ends)])  27 us
    ppermute x8, starting transfers between devices, with_halo(): lax.ppermute(head, axis, [((i + 1) % count, i) for i in range(ends)])  10.3 us
    dot_general x1, matrix products, shards(): jnp.einsum('xyzh,hc->xyzc', hidden, shrink_weight, preferred_element_type...  8.17 us
    concatenate x6, other arithmetic, with_halo(): jnp.concatenate([lax.ppermute(tail, axis, [(i, (i + 1) % count) for i in...  4.91 us
  transfers between devices with their start and end apart: 16, of which 3 were waited for; matrix products, arithmetic and copies ran while one was open for 10% of the time, Pallas kernels for 0%

commit v1 on v0

--- a/solution.py
+++ b/solution.py
@@ -1,7 +1,14 @@
+import functools
+
 import jax
 import jax.numpy as jnp
 from jax import lax
+from jax.experimental import pallas as pl
+from jax.experimental.pallas import tpu as pltpu
 from jax.sharding import PartitionSpec as P
+
+MESH = pl.DeviceIdType.MESH
+reach = 2
 
 product_scale = 8.0
 
@@ -55,17 +62,294 @@
     return jnp.pad(padded, ((0, 0), (1, 1), (0, 0)))
 
 
-def shards(
-    voxels,
-    occupancy,
-    row_weights,
-    column_weights,
-    depth_weights,
-    plane_kernels,
-    expand_weight,
-    shrink_weight,
+def conv_row(window, weight):
+    taps = jnp.dot(weight, window, preferred_element_type=jnp.float32)
+    chans = taps.shape[0] // 3
+    cols = taps.shape[1]
+    lane = lax.broadcasted_iota(jnp.int32, (chans, cols), 1)
+    left = pltpu.roll(taps[:chans], 1, 1)
+    right = pltpu.roll(taps[2 * chans :], cols - 1, 1)
+    left = jnp.where(lane == 0, 0.0, left)
+    right = jnp.where(lane == cols - 1, 0.0, right)
+    return taps[chans : 2 * chans] + left + right
+
+
+def silu(v):
+    return v / (1.0 + jnp.exp(-v))
+
+
+def planes_kernel(
+    n, part, rows_in, weights, yz_out, xy_out, xz_out,
+    pair_in, pair_sum, line_in, yz_plane, yz_inner, row_slots, row_plane, row_inner,
+    pair_s, pair_r, line_s, line_r, halo_s, halo_r, row_s, row_r, spread_s, spread_r, cross_s, cross_r,
 ):
-    features = voxels * occupancy.astype(jnp.bfloat16)[..., None]
+    me = lax.axis_index("gx")
+    g = lax.axis_index("gy")
+    m = n // 2
+    a = me // 2
+    b = me % 2
+    count, chans, cols = part.shape
+    rows = count // n
+
+    def piece(bb, aa):
+        return bb * m + aa + bb * (m - 1 - 2 * aa)
+
+    def owner(j):
+        bb = j // m
+        aa = j % m
+        return (aa + bb * (m - 1 - 2 * aa)) * 2 + bb
+
+    def span(j):
+        return pl.ds(j * rows, rows)
+
+    barrier = pltpu.get_barrier_semaphore()
+    for step in range(1, 2 * n):
+        spot = (me * 2 + g + step) % (2 * n)
+        pl.semaphore_signal(barrier, inc=1, device_id={"gx": spot // 2, "gy": spot % 2}, device_id_type=MESH)
+    pl.semaphore_wait(barrier, 2 * n - 1)
+
+    row_copies = []
+    for dx in range(-reach, reach + 1):
+        for dg in range(2):
+            if dx == 0 and dg == 0:
+                continue
+            slot = reach - dx
+            copy = pltpu.make_async_remote_copy(
+                src_ref=rows_in,
+                dst_ref=row_slots.at[slot, dg],
+                send_sem=row_s.at[slot, dg],
+                recv_sem=row_r.at[slot, dg],
+                device_id={"gx": jnp.clip(me + dx, 0, n - 1), "gy": (g + dg) % 2},
+                device_id_type=MESH,
+            )
+            row_copies.append((dx, copy))
+
+    order = list(range(1, m)) + [0]
+    pair_copies = []
+    for t, off in enumerate(order):
+        aa = (a + off) % m
+        pair_copies.append(
+            pltpu.make_async_remote_copy(
+                src_ref=part.at[span(piece(1 - b, aa))],
+                dst_ref=pair_in.at[t],
+                send_sem=pair_s.at[t],
+                recv_sem=pair_r.at[t],
+                device_id={"gx": a * 2 + 1 - b},
+                device_id_type=MESH,
+            )
+        )
+    pair_copies[0].start()
+    for dx, copy in row_copies:
+        pl.when((me + dx >= 0) & (me + dx < n))(copy.start)
+    for copy in pair_copies[1:]:
+        copy.start()
+
+    line_copies = []
+    for t, off in enumerate(order[:-1]):
+        aa = (a + off) % m
+        pair_copies[t].wait_recv()
+        mine = part[span(piece(b, aa))].astype(jnp.float32)
+        pair_sum[t] = (mine + pair_in[t].astype(jnp.float32)).astype(jnp.bfloat16)
+        copy = pltpu.make_async_remote_copy(
+            src_ref=pair_sum.at[t],
+            dst_ref=line_in.at[t],
+            send_sem=line_s.at[t],
+            recv_sem=line_r.at[t],
+            device_id={"gx": aa * 2 + b},
+            device_id_type=MESH,
+        )
+        copy.start()
+        line_copies.append(copy)
+
+    for dx, copy in row_copies:
+        pl.when((me - dx >= 0) & (me - dx < n))(copy.wait_recv)
+    planes = rows_in.shape[0]
+    for s in range(2 * reach + 1):
+        at = me + s - reach
+        inside = (at >= 0) & (at < n)
+        here = pl.ds(s * chans, chans)
+
+        @pl.when(inside)
+        def _():
+            first = rows_in[...] if s == reach else row_slots[s, 0]
+            total = first.astype(jnp.float32) + row_slots[s, 1].astype(jnp.float32)
+            row_plane[:, here, :] = total.astype(jnp.bfloat16)
+
+        @pl.when(jnp.logical_not(inside))
+        def _():
+            row_plane[:, here, :] = jnp.zeros((planes, chans, cols), jnp.bfloat16)
+
+    for p in range(planes):
+        for s in range(3):
+            at = me + s - 1
+            keep = ((at >= 0) & (at < n)).astype(jnp.float32)
+            inner = silu(conv_row(row_plane[p, s * chans : (s + 3) * chans, :], weights[p, 0]))
+            row_inner[p, s * chans : (s + 1) * chans, :] = (inner * keep).astype(jnp.bfloat16)
+    xy_row = conv_row(row_inner[0], weights[0, 1]).astype(jnp.bfloat16)
+    half = xy_out.shape[1]
+    xy_out[...] = jnp.where(g == 0, xy_row[:, :half], xy_row[:, half:])
+    xz_out[...] = conv_row(row_inner[1], weights[1, 1]).astype(jnp.bfloat16)
+
+    mine_at = piece(b, a)
+    pair_copies[m - 1].wait_recv()
+    for copy in line_copies:
+        copy.wait_recv()
+    total = part[span(mine_at)].astype(jnp.float32) + pair_in[m - 1].astype(jnp.float32)
+    for t in range(m - 1):
+        total = total + line_in[t].astype(jnp.float32)
+    yz_plane[pl.ds(reach * chans, rows * chans), :] = total.astype(jnp.bfloat16).reshape(rows * chans, cols)
+
+    place = g * n + mine_at
+    last = 2 * n - 1
+    edge = reach * chans
+    before = jnp.maximum(place - 1, 0)
+    after = jnp.minimum(place + 1, last)
+    up = pltpu.make_async_remote_copy(
+        src_ref=yz_plane.at[pl.ds(edge, edge)],
+        dst_ref=yz_plane.at[pl.ds(edge + rows * chans, edge)],
+        send_sem=halo_s.at[0],
+        recv_sem=halo_r.at[0],
+        device_id={"gx": owner(before % n), "gy": before // n},
+        device_id_type=MESH,
+    )
+    down = pltpu.make_async_remote_copy(
+        src_ref=yz_plane.at[pl.ds(rows * chans, edge)],
+        dst_ref=yz_plane.at[pl.ds(0, edge)],
+        send_sem=halo_s.at[1],
+        recv_sem=halo_r.at[1],
+        device_id={"gx": owner(after % n), "gy": after // n},
+        device_id_type=MESH,
+    )
+    pl.when(place > 0)(up.start)
+    pl.when(place < last)(down.start)
+
+    @pl.when(place == 0)
+    def _():
+        yz_plane[pl.ds(0, edge), :] = jnp.zeros((edge, cols), jnp.bfloat16)
+
+    @pl.when(place == last)
+    def _():
+        yz_plane[pl.ds(edge + rows * chans, edge), :] = jnp.zeros((edge, cols), jnp.bfloat16)
+
+    def inner_row(i, keep):
+        window = yz_plane[pl.ds(pl.multiple_of(i * chans, chans), 3 * chans), :]
+        inner = silu(conv_row(window, weights[2, 0])) * keep
+        yz_inner[pl.ds(pl.multiple_of(i * chans, chans), chans), :] = inner.astype(jnp.bfloat16)
+
+    for i in range(reach, rows):
+        inner_row(i, 1.0)
+    pl.when(place < last)(up.wait_recv)
+    pl.when(place > 0)(down.wait_recv)
+    for i in list(range(reach)) + list(range(rows, rows + 2)):
+        keep = 1.0
+        if i == 0:
+            keep = (place > 0).astype(jnp.float32)
+        if i == rows + 1:
+            keep = (place < last).astype(jnp.float32)
+        inner_row(i, keep)
+    for r in range(rows):
+        done = conv_row(yz_inner[pl.ds(r * chans, 3 * chans), :], weights[2, 1])
+        yz_out[mine_at * rows + r] = done.astype(jnp.bfloat16)
+
+    def give(j, send, recv, target):
+        return pltpu.make_async_remote_copy(
+            src_ref=yz_out.at[span(j)],
+            dst_ref=yz_out.at[span(j)],
+            send_sem=send,
+            recv_sem=recv,
+            device_id={"gx": target},
+            device_id_type=MESH,
+        )
+
+    partner = a * 2 + 1 - b
+    sends = []
+    for t in range(1, m):
+        copy = give(mine_at, spread_s.at[t], spread_r.at[t], ((a + t) % m) * 2 + b)
+        copy.start()
+        sends.append(copy)
+    copy = give(mine_at, cross_s.at[0], cross_r.at[0], partner)
+    copy.start()
+    sends.append(copy)
+    for t in range(1, m):
+        j = piece(b, (a + m - t) % m)
+        give(j, spread_s.at[t], spread_r.at[t], partner).wait_recv()
+        copy = give(j, cross_s.at[t], cross_r.at[t], partner)
+        copy.start()
+        sends.append(copy)
+    for t in range(m):
+        give(piece(1 - b, (a + m - t) % m), cross_s.at[t], cross_r.at[t], partner).wait_recv()
+    for copy in sends + pair_copies + line_copies:
+        copy.wait_send()
+    for dx, copy in row_copies:
+        pl.when((me + dx >= 0) & (me + dx < n))(copy.wait_send)
+    pl.when(place > 0)(up.wait_send)
+    pl.when(place < last)(down.wait_send)
+
+
+def run_planes(part, rows_in, weights):
+    n = lax.axis_size("gx")
+    m = n // 2
+    count, chans, cols = part.shape
+    rows = count // n
+    planes = rows_in.shape[0]
+    wide = 2 * reach + 1
+    bf = jnp.bfloat16
+    dma = pltpu.SemaphoreType.DMA
+    return pl.pallas_call(
+        functools.partial(planes_kernel, n),
+        out_shape=(
+            jax.ShapeDtypeStruct(part.shape, bf),
+            jax.ShapeDtypeStruct((chans, count), bf),
+            jax.ShapeDtypeStruct((chans, cols), bf),
+        ),
+        in_specs=[pl.BlockSpec(memory_space=pltpu.VMEM)] * 3,
+        out_specs=(pl.BlockSpec(memory_space=pltpu.VMEM),) * 3,
+        scratch_shapes=[
+            pltpu.VMEM((m, rows, chans, cols), bf),
+            pltpu.VMEM((m, rows, chans, cols), bf),
+            pltpu.VMEM((m, rows, chans, cols), bf),
+            pltpu.VMEM(((rows + 4) * chans, cols), bf),
+            pltpu.VMEM(((rows + 2) * chans, cols), bf),
+            pltpu.VMEM((wide, 2, planes, chans, cols), bf),
+            pltpu.VMEM((planes, wide * chans, cols), bf),
+            pltpu.VMEM((planes, 3 * chans, cols), bf),
+            dma((m,)), dma((m,)), dma((m,)), dma((m,)), dma((2,)), dma((2,)),
+            dma((wide, 2)), dma((wide, 2)), dma((m,)), dma((m,)), dma((m,)), dma((m,)),
+        ],
+        compiler_params=pltpu.CompilerParams(collective_id=0, has_side_effects=True),
+    )(part, rows_in, weights)
+
+
+def fits(voxels):
+    n = lax.axis_size("gx")
+    sides = lax.axis_size("gy")
+    xs, ys, zs, _ = voxels.shape
+    return xs == 1 and sides == 2 and n % 2 == 0 and n >= 4 and ys % n == 0 and ys // n >= reach and 2 * ys == zs
+
+
+def fused_planes(features, row_weights, column_weights, depth_weights, plane_kernels):
+    ys = features.shape[1]
+    xy_plane = jnp.einsum(
+        "xyzc,zc->xyc", features, depth_weights, preferred_element_type=jnp.float32
+    )[0].T
+    xz_part = jnp.einsum(
+        "xyzc,yc->xzc", features, column_weights, preferred_element_type=jnp.float32
+    )[0].T
+    part = (features[0].astype(jnp.float32) * row_weights[0].astype(jnp.float32)).astype(jnp.bfloat16)
+    part = part.transpose(0, 2, 1)
+    g = lax.axis_index("gy")
+    blank = jnp.zeros_like(xy_plane)
+    xy_wide = jnp.concatenate(
+        [jnp.where(g == 0, xy_plane, blank), jnp.where(g == 0, blank, xy_plane)], axis=1
+    )
+    rows_in = jnp.stack([xy_wide, xz_part]).astype(jnp.bfloat16)
+    planes, layers, _, _, chans, outs = plane_kernels.shape
+    weights = plane_kernels.transpose(0, 1, 3, 5, 2, 4).reshape(planes, layers, 3 * outs, 3 * chans)
+    yz_out, xy_out, xz_out = run_planes(part, rows_in, weights)
+    return xy_out.T[None], xz_out.T[None], yz_out.transpose(0, 2, 1)
+
+
+def plain_planes(features, row_weights, column_weights, depth_weights, plane_kernels):
     xy_plane = jnp.einsum(
         "xyzc,zc->xyc", features, depth_weights, preferred_element_type=jnp.float32
     ).astype(jnp.bfloat16)
@@ -78,6 +362,22 @@
     xz_out = plane_block(xz_plane, plane_kernels[1], rim_xz)
     yz_plane = lax.psum(yz_part, "gx").astype(jnp.bfloat16)
     yz_out = plane_block(yz_plane, plane_kernels[2], rim_yz)
+    return xy_out, xz_out, yz_out
+
+
+def shards(
+    voxels,
+    occupancy,
+    row_weights,
+    column_weights,
+    depth_weights,
+    plane_kernels,
+    expand_weight,
+    shrink_weight,
+):
+    features = voxels * occupancy.astype(jnp.bfloat16)[..., None]
+    make = fused_planes if fits(voxels) else plain_planes
+    xy_out, xz_out, yz_out = make(features, row_weights, column_weights, depth_weights, plane_kernels)
     product = xy_out.astype(jnp.float32)[:, :, None, :] * xz_out.astype(jnp.float32)[:, None, :, :]
     product = product * yz_out.astype(jnp.float32)[None, :, :, :]
     mixed = (product_scale * product).astype(jnp.bfloat16)

time: 185 us -> 65.9 us (0.36)
  blocking collectives: 95.3 us -> 0 us
  Pallas kernels: 0 us -> 49.3 us
  starting transfers between devices: 37.4 us -> 0 us
  matrix products: 38.9 us -> 6.09 us
  local copies, waits for them, and re-layouts: 1.66 us -> 4.79 us
  other arithmetic: 8.05 us -> 5.23 us
  waiting for transfers between devices: 2.27 us -> 0 us
    psum x2 -> x0, blocking collectives: 95.3 us -> none  [the longest x1 91.9 us: shards(): yz_plane = lax.psum(yz_part, 'gx').astype(jnp.bfloat16)]
    pallas_call x0 -> x1, Pallas kernels: none -> 49.3 us  [run_planes(): pl.pallas_call(functools.partial(planes_kernel, n), out_shape=(jax.ShapeD...]
    ppermute x16 -> x0, starting transfers between devices: 37.4 us -> none  [the longest x8 27 us: with_halo(): lax.ppermute(tail, axis, [(i, (i + 1) % count) for i in range(ends)])]
    dot_general x56 -> x2, matrix products: 30.7 us -> 1.56 us  [the longest x1 0.8 us: fused_planes(): jnp.einsum('xyzc,yc->xzc', features, column_weights, preferred_element_ty...]
    concatenate x6 -> x0, other arithmetic: 4.91 us -> none  [with_halo(): jnp.concatenate([lax.ppermute(tail, axis, [(i, (i + 1) % count) for i in...]
    dot_general x1, matrix products: 8.17 us -> 4.53 us  [shards(): jnp.einsum('xyzh,hc->xyzc', hidden, shrink_weight, preferred_element_type...]
    transpose x0 -> x1, local copies, waits for them, and re-layouts: none -> 2.44 us  [fused_planes(): plane_kernels.transpose(0, 1, 3, 5, 2, 4)]
    ppermute x16 -> x0, waiting for transfers between devices: 2.27 us -> none  [the longest x8 1.88 us: with_halo(): lax.ppermute(head, axis, [((i + 1) % count, i) for i in range(ends)])]
  transfers between devices with their start and end apart: 16 -> 0, of which waited for: 3 -> 0; matrix products, arithmetic and copies ran while one was open for 10% -> 0% of each run, Pallas kernels for 0% -> 0%
where the time goes in v1:
time: 65.9 us; the launch traced here: 65.4 us
  Pallas kernels  49.3 us (75%)
  matrix products  6.09 us (9%)
  other arithmetic  5.23 us (8%)
  local copies, waits for them, and re-layouts  4.79 us (7%)
    pallas_call x1, Pallas kernels, run_planes(): pl.pallas_call(functools.partial(planes_kernel, n), out_shape=(jax.ShapeD...  49.3 us
    dot_general x1, matrix products, shards(): jnp.einsum('xyzh,hc->xyzc', hidden, shrink_weight, preferred_element_type...  4.53 us
    transpose x1, local copies, waits for them, and re-layouts, fused_planes(): plane_kernels.transpose(0, 1, 3, 5, 2, 4)  2.44 us
    transpose x1, other arithmetic, fused_planes(): part = part.transpose(0, 2, 1)  1.62 us
    reshape x1, local copies, waits for them, and re-layouts, fused_planes(): plane_kernels.transpose(0, 1, 3, 5, 2, 4)  1.45 us

profile of v1, /device:TPU:0, one launch (start us, length us, event | category | flops | bytes accessed | tf_op | source)
XLA Modules:
  0.0 65.4 jit_solution(12020005263390707095)
XLA Ops:
  0.0 0.0 copy-start
  0.0 0.7 %bitcast_convert_fusion = f32[64]{0:T(128)S(1)} fusion(bf16[1,64]{1,0:T(2,128)(2,1)} %param.10), kind=kLoop, calls=%fused_computation.28 | loop fusion | flops 64 | bytes 384 | tf_op jit(solution)/shard_map/convert_element_type | solution.py:338
  0.7 0.8 %convert_bitcast_fusion.3 = bf16[64,128]{1,0:T(8,128)(2,1)S(1)} fusion(s32[1,64,128]{2,1,0:T(8,128)} %param.9), kind=kLoop, calls=%fused_computation.27 | loop fusion | flops 8192 | bytes 49152 | tf_op jit(solution)/shard_map/mul | solution.py:378
  1.4 0.8 %copy.16 = bf16[64,64,1]{0,2,1:T(2,128)(2,1)S(1)} copy(bf16[64,64,1]{1,0,2:T(8,128)(2,1)} %bitcast.48) | data formatting | bytes 16384 | tf_op args[3]
  2.2 2.4 %copy.11 = bf16[3,2,3,64,3,64]{5,4,3,2,1,0:T(4,128)(2,1)S(1)} copy(bf16[3,2,3,64,3,64]{3,5,2,4,1,0:T(8,128)(2,1)} %bitcast.45) | data formatting | bytes 884736 | tf_op jit(solution)/shard_map/transpose | solution.py:347
  4.7 0.0 copy-start.1
  4.7 1.5 %reshape.43.weights = bf16[3,2,192,192]{3,2,1,0:T(8,128)(2,1)} reshape(bf16[3,2,3,64,3,64]{5,4,3,2,1,0:T(4,128)(2,1)S(1)} %copy.11) | data formatting | bytes 884736 | tf_op jit(solution)/shard_map/reshape | solution.py:347
  6.2 0.0 copy-done.1
  6.2 1.6 %fusion.4 = (bf16[64,64,128]{2,1,0:T(8,128)(2,1)}, bf16[64,128,64]{1,2,0:T(8,128)(2,1)S(1)}) fusion(f32[64]{0:T(128)S(1)} %bitcast_convert_fusion, bf16[1,64,128,64]{2,3,1,0:T(8,128)(2,1)S(1)} %copy-done.1, bf16[64,128]{1,0:T(8,128)(2,1)S(1)} %convert_bitcast_fusion.3), kind=kLoop, calls=%fused_computation.8 | loop fusion | flops 2097152 | bytes 3162368 | tf_op jit(solution)/shard_map/transpose | solution.py:339
  7.8 0.0 copy-start.2
  7.8 0.8 %fusion.13 = f32[64,1,128]{2,1,0:T(1,128)S(1)} fusion(bf16[64,64,1]{0,2,1:T(2,128)(2,1)S(1)} %copy.16, bf16[64,128,64]{1,2,0:T(8,128)(2,1)S(1)} %get-tuple-element.12), kind=kOutput, calls=%fused_computation.12 | convolution fusion | flops 1048576 | bytes 1089536 | tf_op jit(solution)/shard_map/xyzc,yc->xzc/dot_general | solution.py:335
  8.6 0.0 copy-done.2
  8.6 0.8 %fusion.15 = f32[64,1,64]{2,1,0:T(1,128)S(1)} fusion(bf16[64,128,64]{1,2,0:T(8,128)(2,1)S(1)} %get-tuple-element.12, bf16[128,64,1]{0,1,2:T(8,128)(2,1)S(1)} %bitcast.49), kind=kOutput, calls=%fused_computation.14 | convolution fusion | flops 1048576 | bytes 1081344 | tf_op jit(solution)/shard_map/xyzc,zc->xyc/dot_general | solution.py:332
  9.3 0.0 copy-start.3
  9.4 0.1 maximum_bitcast_fusion
  9.5 0.6 pad_maximum_fusion.rows_in
  10.1 49.3 %shard_map.82 = (bf16[64,64,128]{2,1,0:T(8,128)(2,1)}, bf16[64,64]{1,0:T(8,128)(2,1)}, bf16[64,128]{1,0:T(8,128)(2,1)}) custom-call(bf16[64,64,128]{2,1,0:T(8,128)(2,1)} %get-tuple-element.11.part, bf16[2,64,128]{2,1,0:T(8,128)(2,1)} %pad_maximum_fusion.rows_in, bf16[3,2,192,192]{3,2,1,0:T(8,128)(2,1)} %reshape.43.weights), custom_call_target="tpu_custom_call" | custom-call | tf_op jit(solution)/shard_map/pallas_call | solution.py:298
  59.4 0.7 %convert_bitcast_fusion.1 = f32[64,64]{0,1:T(8,128)S(1)} fusion(bf16[64,64]{1,0:T(8,128)(2,1)} %get-tuple-element.8), kind=kLoop, calls=%fused_computation.20 | loop fusion | flops 4096 | bytes 24576 | tf_op jit(solution)/shard_map/convert_element_type | solution.py:381
  60.1 0.1 copy.12
  60.2 0.7 %convert_bitcast_fusion = f32[128,64]{0,1:T(8,128)S(1)} fusion(bf16[64,128]{1,0:T(8,128)(2,1)} %get-tuple-element.9), kind=kLoop, calls=%fused_computation.19 | loop fusion | flops 8192 | bytes 49152 | tf_op jit(solution)/shard_map/convert_element_type | solution.py:381
  60.9 0.0 copy-done
  60.9 0.0 copy-done.3
  60.9 4.5 %fusion = bf16[1,64,128,64]{2,3,1,0:T(8,128)(2,1)} fusion(bf16[64,64,128]{2,1,0:T(8,128)(2,1)} %get-tuple-element.10, f32[128,64]{0,1:T(8,128)S(1)} %convert_bitcast_fusion, f32[64,64]{1,0:T(8,128)S(1)} %copy.12, bf16[1,64,128,64]{2,3,1,0:T(8,128)(2,1)S(1)} %copy-done.1, bf16[64,128]{1,0:T(8,128)(2,1)S(1)} %convert_bitcast_fusion.3, ...), kind=kOutput, calls=%fused_computation.2 | convolution fusion | flops 279445504 | bytes 3244032 | tf_op jit(solution)/shard_map/xyzh,hc->xyzc/dot_general | solution.py:387
  (2 shorter events, 0.0 us)
Async XLA Ops:
  0.0 60.9 %copy-start = (bf16[128,64]{0,1:T(8,128)(2,1)S(1)}, bf16[128,64]{0,1:T(8,128)(2,1)}, u32[]{:S(2)}) copy-start(bf16[128,64]{0,1:T(8,128)(2,1)} %param.15) | copy-start | bytes 49156
  4.7 1.5 %copy-start.1 = (bf16[1,64,128,64]{2,3,1,0:T(8,128)(2,1)S(1)}, bf16[1,64,128,64]{2,3,1,0:T(8,128)(2,1)}, u32[]{:S(2)}) copy-start(bf16[1,64,128,64]{2,3,1,0:T(8,128)(2,1)} %param.8) | copy-start | bytes 3145732
  7.8 0.8 %copy-start.2 = (bf16[128,64]{0,1:T(8,128)(2,1)S(1)}, bf16[128,64]{0,1:T(8,128)(2,1)}, u32[]{:S(2)}) copy-start(bf16[128,64]{0,1:T(8,128)(2,1)} %param.12) | copy-start | bytes 49156
  9.3 51.6 %copy-start.3 = (bf16[64,128]{1,0:T(8,128)(2,1)S(1)}, bf16[64,128]{1,0:T(8,128)(2,1)}, u32[]{:S(2)}) copy-start(bf16[64,128]{1,0:T(8,128)(2,1)} %param.14) | copy-start | bytes 49156

commit v2 on v1

--- a/solution.py
+++ b/solution.py
@@ -78,8 +78,25 @@
     return v / (1.0 + jnp.exp(-v))
 
 
-def planes_kernel(
-    n, part, rows_in, weights, yz_out, xy_out, xz_out,
+def identity(size):
+    row = lax.broadcasted_iota(jnp.int32, (size, size), 0)
+    col = lax.broadcasted_iota(jnp.int32, (size, size), 1)
+    return jnp.where(row == col, 1.0, 0.0)
+
+
+def flipped(x):
+    eye = identity(x.shape[1]).astype(x.dtype)
+    return lax.dot_general(eye, x, (((1,), (1,)), ((), ())), preferred_element_type=jnp.float32)
+
+
+def column(x, at):
+    lane = lax.broadcasted_iota(jnp.int32, x.shape, 1)
+    return jnp.sum(jnp.where(lane == at, x, 0.0), axis=1, keepdims=True)
+
+
+def block_kernel(
+    n, voxels, occupancy, row_weights, column_weights, depth_weights, plane_kernels, expand, shrink, updated,
+    part, rows_in, weights, wide, yz_out, xy_out, xz_out, row_sums, turned,
     pair_in, pair_sum, line_in, yz_plane, yz_inner, row_slots, row_plane, row_inner,
     pair_s, pair_r, line_s, line_r, halo_s, halo_r, row_s, row_r, spread_s, spread_r, cross_s, cross_r,
 ):
@@ -90,6 +107,10 @@
     b = me % 2
     count, chans, cols = part.shape
     rows = count // n
+    bf = jnp.bfloat16
+
+    def feature_row(y):
+        return voxels[y].astype(jnp.float32) * occupancy[pl.ds(y, 1), :].astype(jnp.float32)
 
     def piece(bb, aa):
         return bb * m + aa + bb * (m - 1 - 2 * aa)
@@ -106,6 +127,25 @@
     for step in range(1, 2 * n):
         spot = (me * 2 + g + step) % (2 * n)
         pl.semaphore_signal(barrier, inc=1, device_id={"gx": spot // 2, "gy": spot % 2}, device_id_type=MESH)
+
+    rw = jnp.broadcast_to(row_weights[...].astype(jnp.float32), (chans, chans))
+    rw = jnp.sum(rw * identity(chans), axis=1, keepdims=True)
+    group = 4 if rows % 4 == 0 else 2
+
+    def yz_terms(step, carry):
+        for k in range(group):
+            y = step * group + k
+            part[y] = (feature_row(y) * rw).astype(bf)
+        return carry
+
+    lax.fori_loop(0, count // group, yz_terms, 0)
+    turned[...] = flipped(column_weights[...])
+    wide[...] = flipped(expand[...]).astype(bf)
+    for p in range(plane_kernels.shape[0]):
+        for layer in range(2):
+            for off in range(3):
+                taps = plane_kernels[p, layer, :, off].reshape(3 * chans, chans)
+                weights[p, layer, off * chans : (off + 1) * chans, :] = flipped(taps).astype(bf)
     pl.semaphore_wait(barrier, 2 * n - 1)
 
     row_copies = []
@@ -138,11 +178,28 @@
                 device_id_type=MESH,
             )
         )
-    pair_copies[0].start()
+    for copy in pair_copies:
+        copy.start()
+
+    row_sums[...] = jnp.zeros(row_sums.shape, jnp.float32)
+    depth = depth_weights[...].astype(jnp.float32)
+    lane = lax.broadcasted_iota(jnp.int32, (chans, cols), 1)
+
+    def row_terms(step, carry):
+        xy, xz = row_sums[0], row_sums[1]
+        for k in range(group):
+            y = step * group + k
+            f = feature_row(y)
+            xy = jnp.where(lane == g * count + y, jnp.sum(f * depth, axis=1, keepdims=True), xy)
+            xz = xz + f * column(turned[...], y)
+        row_sums[0] = xy
+        row_sums[1] = xz
+        return carry
+
+    lax.fori_loop(0, count // group, row_terms, 0)
+    rows_in[...] = row_sums[...].astype(bf)
     for dx, copy in row_copies:
         pl.when((me + dx >= 0) & (me + dx < n))(copy.start)
-    for copy in pair_copies[1:]:
-        copy.start()
 
     line_copies = []
     for t, off in enumerate(order[:-1]):
@@ -185,10 +242,8 @@
             keep = ((at >= 0) & (at < n)).astype(jnp.float32)
             inner = silu(conv_row(row_plane[p, s * chans : (s + 3) * chans, :], weights[p, 0]))
             row_inner[p, s * chans : (s + 1) * chans, :] = (inner * keep).astype(jnp.bfloat16)
-    xy_row = conv_row(row_inner[0], weights[0, 1]).astype(jnp.bfloat16)
-    half = xy_out.shape[1]
-    xy_out[...] = jnp.where(g == 0, xy_row[:, :half], xy_row[:, half:])
-    xz_out[...] = conv_row(row_inner[1], weights[1, 1]).astype(jnp.bfloat16)
+    xy_out[...] = conv_row(row_inner[0], weights[0, 1]).astype(bf).astype(jnp.float32)
+    xz_out[...] = conv_row(row_inner[1], weights[1, 1]).astype(bf).astype(jnp.float32)
 
     mine_at = piece(b, a)
     pair_copies[m - 1].wait_recv()
@@ -261,6 +316,23 @@
             device_id_type=MESH,
         )
 
+    def finish(j):
+        def some_rows(step, carry):
+            at = [j * rows + step * group + k for k in range(group)]
+            mixed = []
+            for y in at:
+                product = column(xy_out[...], g * count + y) * xz_out[...]
+                product = product * yz_out[y].astype(jnp.float32)
+                mixed.append((product_scale * product).astype(bf))
+            mixed = jnp.concatenate(mixed, axis=1)
+            hidden = silu(jnp.dot(wide[...], mixed, preferred_element_type=jnp.float32)).astype(bf)
+            branch = jnp.dot(shrink[...], hidden, preferred_element_type=jnp.float32)
+            for k, y in enumerate(at):
+                updated[y] = (feature_row(y) + branch[:, k * cols : (k + 1) * cols]).astype(bf)
+            return carry
+
+        lax.fori_loop(0, rows // group, some_rows, 0)
+
     partner = a * 2 + 1 - b
     sends = []
     for t in range(1, m):
@@ -270,14 +342,18 @@
     copy = give(mine_at, cross_s.at[0], cross_r.at[0], partner)
     copy.start()
     sends.append(copy)
+    finish(mine_at)
     for t in range(1, m):
         j = piece(b, (a + m - t) % m)
         give(j, spread_s.at[t], spread_r.at[t], partner).wait_recv()
         copy = give(j, cross_s.at[t], cross_r.at[t], partner)
         copy.start()
         sends.append(copy)
+        finish(j)
     for t in range(m):
-        give(piece(1 - b, (a + m - t) % m), cross_s.at[t], cross_r.at[t], partner).wait_recv()
+        j = piece(1 - b, (a + m - t) % m)
+        give(j, cross_s.at[t], cross_r.at[t], partner).wait_recv()
+        finish(j)
     for copy in sends + pair_copies + line_copies:
         copy.wait_send()
     for dx, copy in row_copies:
@@ -286,67 +362,62 @@
     pl.when(place < last)(down.wait_send)
 
 
-def run_planes(part, rows_in, weights):
+def fused(voxels, occupancy, row_weights, column_weights, depth_weights, plane_kernels, expand_weight, shrink_weight):
     n = lax.axis_size("gx")
     m = n // 2
-    count, chans, cols = part.shape
+    count, cols, chans = voxels.shape[1:]
     rows = count // n
-    planes = rows_in.shape[0]
-    wide = 2 * reach + 1
+    sets, layers = plane_kernels.shape[:2]
+    planes = 2
+    span = 2 * reach + 1
     bf = jnp.bfloat16
+    f32 = jnp.float32
     dma = pltpu.SemaphoreType.DMA
-    return pl.pallas_call(
-        functools.partial(planes_kernel, n),
-        out_shape=(
-            jax.ShapeDtypeStruct(part.shape, bf),
-            jax.ShapeDtypeStruct((chans, count), bf),
-            jax.ShapeDtypeStruct((chans, cols), bf),
-        ),
-        in_specs=[pl.BlockSpec(memory_space=pltpu.VMEM)] * 3,
-        out_specs=(pl.BlockSpec(memory_space=pltpu.VMEM),) * 3,
+    updated = pl.pallas_call(
+        functools.partial(block_kernel, n),
+        out_shape=jax.ShapeDtypeStruct((count, chans, cols), bf),
+        in_specs=[pl.BlockSpec(memory_space=pltpu.VMEM)] * 8,
+        out_specs=pl.BlockSpec(memory_space=pltpu.VMEM),
         scratch_shapes=[
+            pltpu.VMEM((count, chans, cols), bf),
+            pltpu.VMEM((planes, chans, cols), bf),
+            pltpu.VMEM((sets, layers, 3 * chans, 3 * chans), bf),
+            pltpu.VMEM(expand_weight.shape[::-1], bf),
+            pltpu.VMEM((count, chans, cols), bf),
+            pltpu.VMEM((chans, 2 * count), f32),
+            pltpu.VMEM((chans, cols), f32),
+            pltpu.VMEM((planes, chans, cols), f32),
+            pltpu.VMEM((chans, count), f32),
             pltpu.VMEM((m, rows, chans, cols), bf),
             pltpu.VMEM((m, rows, chans, cols), bf),
             pltpu.VMEM((m, rows, chans, cols), bf),
             pltpu.VMEM(((rows + 4) * chans, cols), bf),
             pltpu.VMEM(((rows + 2) * chans, cols), bf),
-            pltpu.VMEM((wide, 2, planes, chans, cols), bf),
-            pltpu.VMEM((planes, wide * chans, cols), bf),
+            pltpu.VMEM((span, 2, planes, chans, cols), bf),
+            pltpu.VMEM((planes, span * chans, cols), bf),
             pltpu.VMEM((planes, 3 * chans, cols), bf),
             dma((m,)), dma((m,)), dma((m,)), dma((m,)), dma((2,)), dma((2,)),
-            dma((wide, 2)), dma((wide, 2)), dma((m,)), dma((m,)), dma((m,)), dma((m,)),
+            dma((span, 2)), dma((span, 2)), dma((m,)), dma((m,)), dma((m,)), dma((m,)),
         ],
         compiler_params=pltpu.CompilerParams(collective_id=0, has_side_effects=True),
-    )(part, rows_in, weights)
+    )(
+        voxels[0].transpose(0, 2, 1),
+        occupancy[0],
+        row_weights,
+        column_weights,
+        depth_weights.T,
+        plane_kernels,
+        expand_weight,
+        shrink_weight.T,
+    )
+    return updated.transpose(0, 2, 1)[None]
 
 
 def fits(voxels):
     n = lax.axis_size("gx")
     sides = lax.axis_size("gy")
     xs, ys, zs, _ = voxels.shape
-    return xs == 1 and sides == 2 and n % 2 == 0 and n >= 4 and ys % n == 0 and ys // n >= reach and 2 * ys == zs
-
-
-def fused_planes(features, row_weights, column_weights, depth_weights, plane_kernels):
-    ys = features.shape[1]
-    xy_plane = jnp.einsum(
-        "xyzc,zc->xyc", features, depth_weights, preferred_element_type=jnp.float32
-    )[0].T
-    xz_part = jnp.einsum(
-        "xyzc,yc->xzc", features, column_weights, preferred_element_type=jnp.float32
-    )[0].T
-    part = (features[0].astype(jnp.float32) * row_weights[0].astype(jnp.float32)).astype(jnp.bfloat16)
-    part = part.transpose(0, 2, 1)
-    g = lax.axis_index("gy")
-    blank = jnp.zeros_like(xy_plane)
-    xy_wide = jnp.concatenate(
-        [jnp.where(g == 0, xy_plane, blank), jnp.where(g == 0, blank, xy_plane)], axis=1
-    )
-    rows_in = jnp.stack([xy_wide, xz_part]).astype(jnp.bfloat16)
-    planes, layers, _, _, chans, outs = plane_kernels.shape
-    weights = plane_kernels.transpose(0, 1, 3, 5, 2, 4).reshape(planes, layers, 3 * outs, 3 * chans)
-    yz_out, xy_out, xz_out = run_planes(part, rows_in, weights)
-    return xy_out.T[None], xz_out.T[None], yz_out.transpose(0, 2, 1)
+    return xs == 1 and sides == 2 and n % 2 == 0 and n >= 4 and ys % n == 0 and ys // n >= reach and ys // n % 2 == 0 and 2 * ys == zs
 
 
 def plain_planes(features, row_weights, column_weights, depth_weights, plane_kernels):
@@ -375,9 +446,19 @@
     expand_weight,
     shrink_weight,
 ):
+    if fits(voxels):
+        return fused(
+            voxels,
+            occupancy,
+            row_weights,
+            column_weights,
+            depth_weights,
+            plane_kernels,
+            expand_weight,
+            shrink_weight,
+        )
     features = voxels * occupancy.astype(jnp.bfloat16)[..., None]
-    make = fused_planes if fits(voxels) else plain_planes
-    xy_out, xz_out, yz_out = make(features, row_weights, column_weights, depth_weights, plane_kernels)
+    xy_out, xz_out, yz_out = plain_planes(features, row_weights, column_weights, depth_weights, plane_kernels)
     product = xy_out.astype(jnp.float32)[:, :, None, :] * xz_out.astype(jnp.float32)[:, None, :, :]
     product = product * yz_out.astype(jnp.float32)[None, :, :, :]
     mixed = (product_scale * product).astype(jnp.bfloat16)

time: 65.9 us -> 50.9 us (0.77)
  matrix products: 6.09 us -> 0 us
  other arithmetic: 5.23 us -> 0 us
  local copies, waits for them, and re-layouts: 4.79 us -> 2.26 us
  Pallas kernels: 49.3 us -> 48.5 us
    dot_general x3 -> x0, matrix products: 6.09 us -> none  [the longest x1 4.53 us: shards(): jnp.einsum('xyzh,hc->xyzc', hidden, shrink_weight, preferred_element_type...]
    transpose x1 -> x0, local copies, waits for them, and re-layouts: 2.44 us -> none  [fused_planes(): plane_kernels.transpose(0, 1, 3, 5, 2, 4)]
    convert_element_type x3 -> x0, other arithmetic: 2.12 us -> none  [the longest x1 0.73 us: shards(): xz_out.astype(jnp.float32)[:, None, :, :]]
    transpose x1 -> x0, other arithmetic: 1.62 us -> none  [fused_planes(): part = part.transpose(0, 2, 1)]
    reshape x1 -> x0, local copies, waits for them, and re-layouts: 1.45 us -> none  [fused_planes(): plane_kernels.transpose(0, 1, 3, 5, 2, 4)]
    unnamed x9 -> x1, local copies, waits for them, and re-layouts: 0.82 us -> 2.26 us
    pallas_call x1, Pallas kernels: 49.3 us -> 48.5 us  [fused(): pl.pallas_call(functools.partial(block_kernel, n), out_shape=jax.ShapeDty...]
    mul x1 -> x0, other arithmetic: 0.76 us -> none  [shards(): features = voxels * occupancy.astype(jnp.bfloat16)[..., None]]
where the time goes in v2:
time: 50.9 us; the launch traced here: 50.7 us
  Pallas kernels  48.5 us (95%)
  local copies, waits for them, and re-layouts  2.26 us (4%)
    pallas_call x1, Pallas kernels, fused(): pl.pallas_call(functools.partial(block_kernel, n), out_shape=jax.ShapeDty...  48.5 us
    unnamed x1, local copies, waits for them, and re-layouts  2.26 us

profile of v2, /device:TPU:0, one launch (start us, length us, event | category | flops | bytes accessed | tf_op | source)
XLA Modules:
  0.0 50.7 jit_solution(15668914587274944790)
XLA Ops:
  0.0 48.5 %shard_map.82 = bf16[64,64,128]{2,1,0:T(8,128)(2,1)} custom-call(bf16[64,64,128]{2,1,0:T(8,128)(2,1)} %bitcast.10, s32[64,128]{1,0:T(8,128)} %bitcast.11, bf16[1,64]{1,0:T(2,128)(2,1)} %row_weights.1, bf16[64,64]{1,0:T(8,128)(2,1)} %column_weights.1, bf16[64,128]{1,0:T(8,128)(2,1)} %bitcast.12, bf16[3,2,3,3,64,64]{5,4,3,2,1,0:T(8,128)(2,1)} %plane_kernels.1, ...), custom_call_target="tpu_custom_call" | custom-call | tf_op jit(solution)/shard_map/pallas_call | solution.py:376
  48.5 2.3 %copy.10 = bf16[1,64,128,64]{2,3,1,0:T(8,128)(2,1)} copy(bf16[1,64,128,64]{2,3,1,0:T(8,128)(2,1)} %bitcast.9) | data formatting | bytes 2097152

commit v3 on v2

--- a/solution.py
+++ b/solution.py
@@ -9,6 +9,7 @@
 
 MESH = pl.DeviceIdType.MESH
 reach = 2
+cuts = 2
 
 product_scale = 8.0
 
@@ -97,7 +98,7 @@
 def block_kernel(
     n, voxels, occupancy, row_weights, column_weights, depth_weights, plane_kernels, expand, shrink, updated,
     part, rows_in, weights, wide, yz_out, xy_out, xz_out, row_sums, turned,
-    pair_in, pair_sum, line_in, yz_plane, yz_inner, row_slots, row_plane, row_inner,
+    pair_in, pair_sum, line_in, yz_sum, yz_plane, yz_inner, row_slots, row_plane, row_inner,
     pair_s, pair_r, line_s, line_r, halo_s, halo_r, row_s, row_r, spread_s, spread_r, cross_s, cross_r,
 ):
     me = lax.axis_index("gx")
@@ -139,13 +140,6 @@
         return carry
 
     lax.fori_loop(0, count // group, yz_terms, 0)
-    turned[...] = flipped(column_weights[...])
-    wide[...] = flipped(expand[...]).astype(bf)
-    for p in range(plane_kernels.shape[0]):
-        for layer in range(2):
-            for off in range(3):
-                taps = plane_kernels[p, layer, :, off].reshape(3 * chans, chans)
-                weights[p, layer, off * chans : (off + 1) * chans, :] = flipped(taps).astype(bf)
     pl.semaphore_wait(barrier, 2 * n - 1)
 
     row_copies = []
@@ -164,22 +158,60 @@
             )
             row_copies.append((dx, copy))
 
-    order = list(range(1, m)) + [0]
-    pair_copies = []
-    for t, off in enumerate(order):
-        aa = (a + off) % m
-        pair_copies.append(
-            pltpu.make_async_remote_copy(
-                src_ref=part.at[span(piece(1 - b, aa))],
-                dst_ref=pair_in.at[t],
-                send_sem=pair_s.at[t],
-                recv_sem=pair_r.at[t],
-                device_id={"gx": a * 2 + 1 - b},
+    sub = rows // cuts
+    far = sorted([d for d in range(1 - m, m) if d != 0], key=lambda d: -abs(d))
+    near = far[::-1]
+    partner = a * 2 + 1 - b
+
+    def valid(d):
+        return (a + d >= 0) & (a + d < m)
+
+    def spot(d):
+        return jnp.clip(a + d, 0, m - 1)
+
+    def sub_span(j, h):
+        return pl.ds(j * rows + h * sub, sub)
+
+    pair_copies = {}
+    line_copies = {}
+    for d in far + [0]:
+        for h in range(cuts):
+            pair_copies[d, h] = pltpu.make_async_remote_copy(
+                src_ref=part.at[sub_span(piece(1 - b, spot(d)), h)],
+                dst_ref=pair_in.at[d + m - 1, h],
+                send_sem=pair_s.at[d + m - 1, h],
+                recv_sem=pair_r.at[d + m - 1, h],
+                device_id={"gx": partner},
                 device_id_type=MESH,
             )
-        )
-    for copy in pair_copies:
-        copy.start()
+            if d != 0:
+                line_copies[d, h] = pltpu.make_async_remote_copy(
+                    src_ref=pair_sum.at[d + m - 1, h],
+                    dst_ref=line_in.at[d + m - 1, h],
+                    send_sem=line_s.at[d + m - 1, h],
+                    recv_sem=line_r.at[d + m - 1, h],
+                    device_id={"gx": spot(d) * 2 + b},
+                    device_id_type=MESH,
+                )
+    for (d, h), copy in pair_copies.items():
+        pl.when(valid(d))(copy.start)
+    for d in far:
+        for h in range(cuts):
+
+            @pl.when(valid(d))
+            def _():
+                pair_copies[d, h].wait_recv()
+                mine = part[sub_span(piece(b, spot(d)), h)].astype(jnp.float32)
+                pair_sum[d + m - 1, h] = (mine + pair_in[d + m - 1, h].astype(jnp.float32)).astype(bf)
+                line_copies[d, h].start()
+
+    turned[...] = flipped(column_weights[...])
+    wide[...] = flipped(expand[...]).astype(bf)
+    for p in range(plane_kernels.shape[0]):
+        for layer in range(2):
+            for off in range(3):
+                taps = plane_kernels[p, layer, :, off].reshape(3 * chans, chans)
+                weights[p, layer, off * chans : (off + 1) * chans, :] = flipped(taps).astype(bf)
 
     row_sums[...] = jnp.zeros(row_sums.shape, jnp.float32)
     depth = depth_weights[...].astype(jnp.float32)
@@ -198,61 +230,22 @@
 
     lax.fori_loop(0, count // group, row_terms, 0)
     rows_in[...] = row_sums[...].astype(bf)
-    for dx, copy in row_copies:
-        pl.when((me + dx >= 0) & (me + dx < n))(copy.start)
-
-    line_copies = []
-    for t, off in enumerate(order[:-1]):
-        aa = (a + off) % m
-        pair_copies[t].wait_recv()
-        mine = part[span(piece(b, aa))].astype(jnp.float32)
-        pair_sum[t] = (mine + pair_in[t].astype(jnp.float32)).astype(jnp.bfloat16)
-        copy = pltpu.make_async_remote_copy(
-            src_ref=pair_sum.at[t],
-            dst_ref=line_in.at[t],
-            send_sem=line_s.at[t],
-            recv_sem=line_r.at[t],
-            device_id={"gx": aa * 2 + b},
-            device_id_type=MESH,
-        )
-        copy.start()
-        line_copies.append(copy)
-
-    for dx, copy in row_copies:
-        pl.when((me - dx >= 0) & (me - dx < n))(copy.wait_recv)
-    planes = rows_in.shape[0]
-    for s in range(2 * reach + 1):
-        at = me + s - reach
-        inside = (at >= 0) & (at < n)
-        here = pl.ds(s * chans, chans)
-
-        @pl.when(inside)
-        def _():
-            first = rows_in[...] if s == reach else row_slots[s, 0]
-            total = first.astype(jnp.float32) + row_slots[s, 1].astype(jnp.float32)
-            row_plane[:, here, :] = total.astype(jnp.bfloat16)
-
-        @pl.when(jnp.logical_not(inside))
-        def _():
-            row_plane[:, here, :] = jnp.zeros((planes, chans, cols), jnp.bfloat16)
-
-    for p in range(planes):
-        for s in range(3):
-            at = me + s - 1
-            keep = ((at >= 0) & (at < n)).astype(jnp.float32)
-            inner = silu(conv_row(row_plane[p, s * chans : (s + 3) * chans, :], weights[p, 0]))
-            row_inner[p, s * chans : (s + 1) * chans, :] = (inner * keep).astype(jnp.bfloat16)
-    xy_out[...] = conv_row(row_inner[0], weights[0, 1]).astype(bf).astype(jnp.float32)
-    xz_out[...] = conv_row(row_inner[1], weights[1, 1]).astype(bf).astype(jnp.float32)
-
     mine_at = piece(b, a)
-    pair_copies[m - 1].wait_recv()
-    for copy in line_copies:
-        copy.wait_recv()
-    total = part[span(mine_at)].astype(jnp.float32) + pair_in[m - 1].astype(jnp.float32)
-    for t in range(m - 1):
-        total = total + line_in[t].astype(jnp.float32)
-    yz_plane[pl.ds(reach * chans, rows * chans), :] = total.astype(jnp.bfloat16).reshape(rows * chans, cols)
+    for h in range(cuts):
+        at = pl.ds(h * sub, sub)
+        pair_copies[0, h].wait_recv()
+        mine = part[sub_span(mine_at, h)].astype(jnp.float32)
+        yz_sum[at] = mine + pair_in[m - 1, h].astype(jnp.float32)
+    for d in near:
+        for h in range(cuts):
+
+            @pl.when(valid(-d))
+            def _():
+                at = pl.ds(h * sub, sub)
+                line_copies[d, h].wait_recv()
+                yz_sum[at] = yz_sum[at] + line_in[d + m - 1, h].astype(jnp.float32)
+
+    yz_plane[pl.ds(reach * chans, rows * chans), :] = yz_sum[...].astype(bf).reshape(rows * chans, cols)
 
     place = g * n + mine_at
     last = 2 * n - 1
@@ -277,6 +270,8 @@
     )
     pl.when(place > 0)(up.start)
     pl.when(place < last)(down.start)
+    for dx, copy in row_copies:
+        pl.when((me + dx >= 0) & (me + dx < n))(copy.start)
 
     @pl.when(place == 0)
     def _():
@@ -302,23 +297,63 @@
         if i == rows + 1:
             keep = (place < last).astype(jnp.float32)
         inner_row(i, keep)
-    for r in range(rows):
-        done = conv_row(yz_inner[pl.ds(r * chans, 3 * chans), :], weights[2, 1])
-        yz_out[mine_at * rows + r] = done.astype(jnp.bfloat16)
-
-    def give(j, send, recv, target):
+    def give(j, h, sems, at, target):
         return pltpu.make_async_remote_copy(
-            src_ref=yz_out.at[span(j)],
-            dst_ref=yz_out.at[span(j)],
-            send_sem=send,
-            recv_sem=recv,
+            src_ref=yz_out.at[sub_span(j, h)],
+            dst_ref=yz_out.at[sub_span(j, h)],
+            send_sem=sems[0].at[at, h],
+            recv_sem=sems[1].at[at, h],
             device_id={"gx": target},
             device_id_type=MESH,
         )
 
-    def finish(j):
+    spread = (spread_s, spread_r)
+    cross = (cross_s, cross_r)
+    sends = []
+    for h in range(cuts):
+        for r in range(h * sub, (h + 1) * sub):
+            done = conv_row(yz_inner[pl.ds(r * chans, 3 * chans), :], weights[2, 1])
+            yz_out[mine_at * rows + r] = done.astype(bf)
+        for d in far:
+            copy = give(mine_at, h, spread, d + m - 1, spot(d) * 2 + b)
+            pl.when(valid(d))(copy.start)
+            sends.append((d, copy))
+        copy = give(mine_at, h, cross, m - 1, partner)
+        copy.start()
+        sends.append((0, copy))
+
+    for dx, copy in row_copies:
+        pl.when((me - dx >= 0) & (me - dx < n))(copy.wait_recv)
+    planes = rows_in.shape[0]
+    for s in range(2 * reach + 1):
+        at = me + s - reach
+        inside = (at >= 0) & (at < n)
+        here = pl.ds(s * chans, chans)
+
+        @pl.when(inside)
+        def _():
+            first = rows_in[...] if s == reach else row_slots[s, 0]
+            total = first.astype(jnp.float32) + row_slots[s, 1].astype(jnp.float32)
+            row_plane[:, here, :] = total.astype(jnp.bfloat16)
+
+        @pl.when(jnp.logical_not(inside))
+        def _():
+            row_plane[:, here, :] = jnp.zeros((planes, chans, cols), jnp.bfloat16)
+
+    for p in range(planes):
+        for s in range(3):
+            at = me + s - 1
+            keep = ((at >= 0) & (at < n)).astype(jnp.float32)
+            inner = silu(conv_row(row_plane[p, s * chans : (s + 3) * chans, :], weights[p, 0]))
+            row_inner[p, s * chans : (s + 1) * chans, :] = (inner * keep).astype(jnp.bfloat16)
+    xy_out[...] = conv_row(row_inner[0], weights[0, 1]).astype(bf).astype(jnp.float32)
+    xz_out[...] = conv_row(row_inner[1], weights[1, 1]).astype(bf).astype(jnp.float32)
+
+    step_rows = 4 if sub % 4 == 0 else (2 if sub % 2 == 0 else 1)
+
+    def finish(j, h):
         def some_rows(step, carry):
-            at = [j * rows + step * group + k for k in range(group)]
+            at = [j * rows + h * sub + step * step_rows + k for k in range(step_rows)]
             mixed = []
             for y in at:
                 product = column(xy_out[...], g * count + y) * xz_out[...]
@@ -331,31 +366,36 @@
                 updated[y] = (feature_row(y) + branch[:, k * cols : (k + 1) * cols]).astype(bf)
             return carry
 
-        lax.fori_loop(0, rows // group, some_rows, 0)
-
-    partner = a * 2 + 1 - b
-    sends = []
-    for t in range(1, m):
-        copy = give(mine_at, spread_s.at[t], spread_r.at[t], ((a + t) % m) * 2 + b)
-        copy.start()
-        sends.append(copy)
-    copy = give(mine_at, cross_s.at[0], cross_r.at[0], partner)
-    copy.start()
-    sends.append(copy)
-    finish(mine_at)
-    for t in range(1, m):
-        j = piece(b, (a + m - t) % m)
-        give(j, spread_s.at[t], spread_r.at[t], partner).wait_recv()
-        copy = give(j, cross_s.at[t], cross_r.at[t], partner)
-        copy.start()
-        sends.append(copy)
-        finish(j)
-    for t in range(m):
-        j = piece(1 - b, (a + m - t) % m)
-        give(j, cross_s.at[t], cross_r.at[t], partner).wait_recv()
-        finish(j)
-    for copy in sends + pair_copies + line_copies:
-        copy.wait_send()
+        lax.fori_loop(0, sub // step_rows, some_rows, 0)
+
+    for h in range(cuts):
+        finish(mine_at, h)
+    for d in near:
+        for h in range(cuts):
+
+            @pl.when(valid(d))
+            def _():
+                j = piece(b, spot(d))
+                give(j, h, spread, m - 1 - d, partner).wait_recv()
+                give(j, h, cross, m - 1 + d, partner).start()
+                finish(j, h)
+
+    for d in [0] + near:
+        for h in range(cuts):
+
+            @pl.when(valid(d))
+            def _():
+                j = piece(1 - b, spot(d))
+                give(j, h, cross, m - 1 + d, partner).wait_recv()
+                finish(j, h)
+
+    for d in near:
+        for h in range(cuts):
+            pl.when(valid(d))(give(piece(b, spot(d)), h, cross, m - 1 + d, partner).wait_send)
+    for d, copy in sends:
+        pl.when(valid(d))(copy.wait_send)
+    for (d, h), copy in list(pair_copies.items()) + list(line_copies.items()):
+        pl.when(valid(d))(copy.wait_send)
     for dx, copy in row_copies:
         pl.when((me + dx >= 0) & (me + dx < n))(copy.wait_send)
     pl.when(place > 0)(up.wait_send)
@@ -373,9 +413,10 @@
     bf = jnp.bfloat16
     f32 = jnp.float32
     dma = pltpu.SemaphoreType.DMA
+    block = dma((2 * m - 1, cuts))
     updated = pl.pallas_call(
         functools.partial(block_kernel, n),
-        out_shape=jax.ShapeDtypeStruct((count, chans, cols), bf),
+        out_shape=pltpu.VMEM((count, chans, cols), bf),
         in_specs=[pl.BlockSpec(memory_space=pltpu.VMEM)] * 8,
         out_specs=pl.BlockSpec(memory_space=pltpu.VMEM),
         scratch_shapes=[
@@ -388,16 +429,17 @@
             pltpu.VMEM((chans, cols), f32),
             pltpu.VMEM((planes, chans, cols), f32),
             pltpu.VMEM((chans, count), f32),
-            pltpu.VMEM((m, rows, chans, cols), bf),
-            pltpu.VMEM((m, rows, chans, cols), bf),
-            pltpu.VMEM((m, rows, chans, cols), bf),
+            pltpu.VMEM((2 * m - 1, cuts, rows // cuts, chans, cols), bf),
+            pltpu.VMEM((2 * m - 1, cuts, rows // cuts, chans, cols), bf),
+            pltpu.VMEM((2 * m - 1, cuts, rows // cuts, chans, cols), bf),
+            pltpu.VMEM((rows, chans, cols), f32),
             pltpu.VMEM(((rows + 4) * chans, cols), bf),
             pltpu.VMEM(((rows + 2) * chans, cols), bf),
             pltpu.VMEM((span, 2, planes, chans, cols), bf),
             pltpu.VMEM((planes, span * chans, cols), bf),
             pltpu.VMEM((planes, 3 * chans, cols), bf),
-            dma((m,)), dma((m,)), dma((m,)), dma((m,)), dma((2,)), dma((2,)),
-            dma((span, 2)), dma((span, 2)), dma((m,)), dma((m,)), dma((m,)), dma((m,)),
+            block, block, block, block, dma((2,)), dma((2,)),
+            dma((span, 2)), dma((span, 2)), block, block, block, block,
         ],
         compiler_params=pltpu.CompilerParams(collective_id=0, has_side_effects=True),
     )(
@@ -417,7 +459,7 @@
     n = lax.axis_size("gx")
     sides = lax.axis_size("gy")
     xs, ys, zs, _ = voxels.shape
-    return xs == 1 and sides == 2 and n % 2 == 0 and n >= 4 and ys % n == 0 and ys // n >= reach and ys // n % 2 == 0 and 2 * ys == zs
+    return xs == 1 and sides == 2 and n % 2 == 0 and n >= 4 and ys % n == 0 and ys // n >= reach and ys // n % cuts == 0 and 2 * ys == zs
 
 
 def plain_planes(features, row_weights, column_weights, depth_weights, plane_kernels):

time: 50.9 us -> 47.5 us (0.933)
  the two profiles are of different devices: /device:TPU:0 before, /device:TPU:8 now
where the time goes in v3:
time: 47.5 us; the launch traced here: 47.4 us
  Pallas kernels  46.4 us (98%)
  local copies, waits for them, and re-layouts  0.97 us (2%)
    pallas_call x1, Pallas kernels, fused(): pl.pallas_call(functools.partial(block_kernel, n), out_shape=pltpu.VMEM((...  46.4 us
    unnamed x1, local copies, waits for them, and re-layouts  0.97 us

profile of v3, /device:TPU:8, one launch (start us, length us, event | category | flops | bytes accessed | tf_op | source)
XLA Modules:
  0.0 47.4 jit_solution(982256710378370571)
XLA Ops:
  0.0 46.4 %shard_map.82 = bf16[64,64,128]{2,1,0:T(8,128)(2,1)S(1)} custom-call(bf16[64,64,128]{2,1,0:T(8,128)(2,1)} %bitcast.10, s32[64,128]{1,0:T(8,128)} %bitcast.11, bf16[1,64]{1,0:T(2,128)(2,1)} %row_weights.1, bf16[64,64]{1,0:T(8,128)(2,1)} %column_weights.1, bf16[64,128]{1,0:T(8,128)(2,1)} %bitcast.12, bf16[3,2,3,3,64,64]{5,4,3,2,1,0:T(8,128)(2,1)} %plane_kernels.1, ...), custom_call_target="tpu_custom_call" | custom-call | tf_op jit(solution)/shard_map/pallas_call | solution.py:417
  46.4 1.0 %copy.10 = bf16[1,64,128,64]{2,3,1,0:T(8,128)(2,1)} copy(bf16[1,64,128,64]{2,3,1,0:T(8,128)(2,1)S(1)} %bitcast.9) | data formatting | bytes 2097152

commit v4 on v3

--- a/solution.py
+++ b/solution.py
@@ -314,7 +314,7 @@
         for r in range(h * sub, (h + 1) * sub):
             done = conv_row(yz_inner[pl.ds(r * chans, 3 * chans), :], weights[2, 1])
             yz_out[mine_at * rows + r] = done.astype(bf)
-        for d in far:
+        for d in near:
             copy = give(mine_at, h, spread, d + m - 1, spot(d) * 2 + b)
             pl.when(valid(d))(copy.start)
             sends.append((d, copy))
@@ -370,8 +370,8 @@
 
     for h in range(cuts):
         finish(mine_at, h)
-    for d in near:
-        for h in range(cuts):
+    for h in range(cuts):
+        for d in near:
 
             @pl.when(valid(d))
             def _():
@@ -380,8 +380,8 @@
                 give(j, h, cross, m - 1 + d, partner).start()
                 finish(j, h)
 
-    for d in [0] + near:
-        for h in range(cuts):
+    for h in range(cuts):
+        for d in [0] + near:
 
             @pl.when(valid(d))
             def _():

time: 47.5 us -> 46.8 us (0.985)
  the two profiles are of different devices: /device:TPU:8 before, /device:TPU:0 now
where the time goes in v4:
time: 46.8 us; the launch traced here: 46.7 us
  Pallas kernels  45.7 us (98%)
  local copies, waits for them, and re-layouts  0.97 us (2%)
    pallas_call x1, Pallas kernels, fused(): pl.pallas_call(functools.partial(block_kernel, n), out_shape=pltpu.VMEM((...  45.7 us
    unnamed x1, local copies, waits for them, and re-layouts  0.97 us

profile of v4, /device:TPU:0, one launch (start us, length us, event | category | flops | bytes accessed | tf_op | source)
XLA Modules:
  0.0 46.7 jit_solution(11040442209663122287)
XLA Ops:
  0.0 45.7 %shard_map.82 = bf16[64,64,128]{2,1,0:T(8,128)(2,1)S(1)} custom-call(bf16[64,64,128]{2,1,0:T(8,128)(2,1)} %bitcast.10, s32[64,128]{1,0:T(8,128)} %bitcast.11, bf16[1,64]{1,0:T(2,128)(2,1)} %row_weights.1, bf16[64,64]{1,0:T(8,128)(2,1)} %column_weights.1, bf16[64,128]{1,0:T(8,128)(2,1)} %bitcast.12, bf16[3,2,3,3,64,64]{5,4,3,2,1,0:T(8,128)(2,1)} %plane_kernels.1, ...), custom_call_target="tpu_custom_call" | custom-call | tf_op jit(solution)/shard_map/pallas_call | solution.py:417
  45.7 1.0 %copy.10 = bf16[1,64,128,64]{2,3,1,0:T(8,128)(2,1)} copy(bf16[1,64,128,64]{2,3,1,0:T(8,128)(2,1)S(1)} %bitcast.9) | data formatting | bytes 2097152

commit v5 on v4

--- a/solution.py
+++ b/solution.py
@@ -96,7 +96,8 @@
 
 
 def block_kernel(
-    n, voxels, occupancy, row_weights, column_weights, depth_weights, plane_kernels, expand, shrink, updated,
+    n, voxels, occupancy, row_weights, column_weights, depth_weights, kernels_in, expand, shrink, updated,
+    plane_kernels, fetch_s,
     part, rows_in, weights, wide, yz_out, xy_out, xz_out, row_sums, turned,
     pair_in, pair_sum, line_in, yz_sum, yz_plane, yz_inner, row_slots, row_plane, row_inner,
     pair_s, pair_r, line_s, line_r, halo_s, halo_r, row_s, row_r, spread_s, spread_r, cross_s, cross_r,
@@ -124,6 +125,8 @@
     def span(j):
         return pl.ds(j * rows, rows)
 
+    fetch = pltpu.make_async_copy(kernels_in, plane_kernels, fetch_s)
+    fetch.start()
     barrier = pltpu.get_barrier_semaphore()
     for step in range(1, 2 * n):
         spot = (me * 2 + g + step) % (2 * n)
@@ -205,6 +208,7 @@
                 pair_sum[d + m - 1, h] = (mine + pair_in[d + m - 1, h].astype(jnp.float32)).astype(bf)
                 line_copies[d, h].start()
 
+    fetch.wait()
     turned[...] = flipped(column_weights[...])
     wide[...] = flipped(expand[...]).astype(bf)
     for p in range(plane_kernels.shape[0]):
@@ -417,9 +421,11 @@
     updated = pl.pallas_call(
         functools.partial(block_kernel, n),
         out_shape=pltpu.VMEM((count, chans, cols), bf),
-        in_specs=[pl.BlockSpec(memory_space=pltpu.VMEM)] * 8,
+        in_specs=[pl.BlockSpec(memory_space=pl.ANY if k == 5 else pltpu.VMEM) for k in range(8)],
         out_specs=pl.BlockSpec(memory_space=pltpu.VMEM),
         scratch_shapes=[
+            pltpu.VMEM(plane_kernels.shape, bf),
+            dma,
             pltpu.VMEM((count, chans, cols), bf),
             pltpu.VMEM((planes, chans, cols), bf),
             pltpu.VMEM((sets, layers, 3 * chans, 3 * chans), bf),

time: 46.8 us -> 46.6 us (level)
  no operation moved by 1% of the time
where the time goes in v5:
time: 46.6 us; the launch traced here: 46.4 us
  Pallas kernels  45.5 us (98%)
  local copies, waits for them, and re-layouts  0.97 us (2%)
    pallas_call x1, Pallas kernels, fused(): pl.pallas_call(functools.partial(block_kernel, n), out_shape=pltpu.VMEM((...  45.5 us
    unnamed x1, local copies, waits for them, and re-layouts  0.97 us

profile of v5, /device:TPU:0, one launch (start us, length us, event | category | flops | bytes accessed | tf_op | source)
XLA Modules:
  0.0 46.4 jit_solution(915742447559301888)
XLA Ops:
  0.0 45.5 %shard_map.82 = bf16[64,64,128]{2,1,0:T(8,128)(2,1)S(1)} custom-call(bf16[64,64,128]{2,1,0:T(8,128)(2,1)} %bitcast.10, s32[64,128]{1,0:T(8,128)} %bitcast.11, bf16[1,64]{1,0:T(2,128)(2,1)} %row_weights.1, bf16[64,64]{1,0:T(8,128)(2,1)} %column_weights.1, bf16[64,128]{1,0:T(8,128)(2,1)} %bitcast.12, bf16[3,2,3,3,64,64]{5,4,3,2,1,0:T(8,128)(2,1)} %kernels_in.1, ...), custom_call_target="tpu_custom_call" | custom-call | tf_op jit(solution)/shard_map/pallas_call | solution.py:421
  45.5 1.0 %copy.10 = bf16[1,64,128,64]{2,3,1,0:T(8,128)(2,1)} copy(bf16[1,64,128,64]{2,3,1,0:T(8,128)(2,1)S(1)} %bitcast.9) | data formatting | bytes 2097152
